TPU v7x, 512 devices: a whole 4x8x8 slice. The times are simulated.
512 devices in a mesh: seq: 32 (over x, y), chan: 16 (over z, core).
Axes of the slice: x: 4, y: 8, z: 8, core: 2. Of those that a mesh axis runs over, the one named last changes fastest.
Arguments:
- tokens: bfloat16 [1536, 16384], P('chan', 'seq'), may hold values from -6 to 6
- gate_weight: bfloat16 [1536, 1536], P('chan'), may hold values from -0.15625 to 0.15625
- value_weight: bfloat16 [1536, 1536], P('chan'), may hold values from -0.15625 to 0.15625
- first_factor: bfloat16 [64, 256, 256], P('seq'), may hold values from -0.375 to 0.375
- second_factor: bfloat16 [256, 64, 64], P('seq'), may hold values from -0.75 to 0.75
- down_latent: bfloat16 [1536, 128], P('chan'), may hold values from -0.15625 to 0.15625
- up_latent: bfloat16 [1536, 128], P('chan'), may hold values from -0.5 to 0.5
- doc_lengths: int32 [64], replicated, may hold values from 1 to 8704, 16384 in all
- cotangent: bfloat16 [1536, 16384], P('chan', 'seq'), may hold values from -6 to 6
Outputs:
- hidden: bfloat16 [1536, 16384], P('chan', 'seq')
- d_gate_weight: float32 [1536, 1536], P('chan')
- d_value_weight: float32 [1536, 1536], P('chan')
- d_first: float32 [64, 256, 256], P('seq', 'chan')
- d_second: float32 [256, 64, 64], P('seq', 'chan')
- d_down: float32 [1536, 128], P('chan')
- d_up: float32 [1536, 128], P('chan')
Inputs may be any that keep to these rules, and one draw needn't show every extreme that they name: `doc_lengths`: the documents' lengths sum to 16384; the longest is exactly 8704 tokens.
All inputs are finite; a program needn't handle non-finite values.
Results may differ from a plain program's by a relative error of at most 0.0058.
Values may be sent and summed in bfloat16 or wider, within the bound.
No kernel may reach another device: no remote copies, remote signals or barrier semaphores. Data moves between devices by JAX's collectives and lax.ppermute only.
A program may use at most 64 MiB of HBM per device.

v0:
```python
import jax
import jax.numpy as jnp
from jax import lax
from jax.sharding import PartitionSpec as P


def body(
    tokens,
    gate_weight,
    value_weight,
    first_factor,
    second_factor,
    down_latent,
    up_latent,
    doc_lengths,
    cotangent,
):
    highest = lax.Precision.HIGHEST
    chan_rows, tok_cols = tokens.shape
    block_width = first_factor.shape[1]
    blocks_here = tok_cols // block_width
    gathered = lax.all_gather(tokens, "chan", axis=0, tiled=True)
    gate_pre = jnp.dot(gate_weight, gathered, preferred_element_type=jnp.float32)
    value_acc = jnp.dot(value_weight, gathered, preferred_element_type=jnp.float32)
    value_bf = value_acc.astype(jnp.bfloat16)
    doc_ends = jnp.cumsum(doc_lengths)
    doc_begins = doc_ends - doc_lengths
    position = lax.axis_index("seq") * tok_cols + jnp.arange(tok_cols, dtype=jnp.int32)
    member = (
        (position[None, :] >= doc_begins[:, None]) & (position[None, :] < doc_ends[:, None])
    ).astype(jnp.float32)
    len_scale = lax.rsqrt(doc_lengths.astype(jnp.float32))
    latent_part = jnp.einsum("ct,cl->lt", tokens, down_latent, preferred_element_type=jnp.float32)
    latent_full = lax.psum(latent_part, "chan")
    doc_sums = lax.psum(jnp.einsum("dt,lt->dl", member, latent_full, precision=highest), "seq")
    pooled = doc_sums * len_scale[:, None]
    up_float = up_latent.astype(jnp.float32)
    spread_rows = jnp.einsum("cl,dl->cd", up_float, pooled, precision=highest)
    summary = jnp.dot(spread_rows, member, precision=highest)
    blocked = value_bf.reshape(chan_rows, blocks_here, block_width)
    inner_mix = jnp.einsum(
        "ikj,cij->kic", first_factor, blocked, preferred_element_type=jnp.float32
    ).astype(jnp.bfloat16)
    columns = lax.all_to_all(inner_mix, "seq", split_axis=0, concat_axis=1, tiled=True)
    outer_mix = jnp.einsum(
        "kmi,kic->kmc", second_factor, columns, preferred_element_type=jnp.float32
    ).astype(jnp.bfloat16)
    mixed_back = lax.all_to_all(outer_mix, "seq", split_axis=1, concat_axis=0, tiled=True)
    mixed = (
        jnp.transpose(mixed_back, (2, 1, 0)).reshape(chan_rows, tok_cols).astype(jnp.float32)
        + summary
    )
    sig = jax.nn.sigmoid(gate_pre)
    act = gate_pre * sig
    hidden = (act * mixed).astype(jnp.bfloat16)
    upstream = cotangent.astype(jnp.float32)
    d_mixed = upstream * act
    d_mixed_bf = d_mixed.astype(jnp.bfloat16)
    d_gate_bf = (upstream * mixed * sig * (1.0 + gate_pre * (1.0 - sig))).astype(jnp.bfloat16)
    d_send = jnp.transpose(d_mixed_bf.reshape(chan_rows, blocks_here, block_width), (2, 1, 0))
    d_outer = lax.all_to_all(d_send, "seq", split_axis=0, concat_axis=1, tiled=True)
    d_inner = jnp.einsum(
        "kmi,kmc->kic", second_factor, d_outer, preferred_element_type=jnp.float32
    ).astype(jnp.bfloat16)
    d_second_part = jnp.einsum("kmc,kic->kmi", d_outer, columns, preferred_element_type=jnp.float32)
    d_rows = lax.all_to_all(d_inner, "seq", split_axis=1, concat_axis=0, tiled=True)
    d_value_bf = (
        jnp.einsum("ikj,kic->cij", first_factor, d_rows, preferred_element_type=jnp.float32)
        .astype(jnp.bfloat16)
        .reshape(chan_rows, tok_cols)
    )
    d_first_part = jnp.einsum("kic,cij->ikj", d_rows, blocked, preferred_element_type=jnp.float32)
    per_doc = jnp.einsum("ct,dt->cd", d_mixed, member, precision=highest)
    d_up_part = jnp.einsum("cd,dl->cl", per_doc, pooled, precision=highest)
    d_pooled = lax.psum(
        jnp.einsum("cd,cl->dl", per_doc, up_float, precision=highest), ("seq", "chan")
    )
    d_latent_bf = jnp.einsum(
        "dl,dt->lt", d_pooled * len_scale[:, None], member, precision=highest
    ).astype(jnp.bfloat16)
    d_down_part = jnp.einsum("ct,lt->cl", tokens, d_latent_bf, preferred_element_type=jnp.float32)
    both_grads = jnp.concatenate([d_gate_bf, d_value_bf], axis=0)
    d_proj = jnp.einsum("ot,it->oi", both_grads, gathered, preferred_element_type=jnp.float32)
    d_proj, d_down, d_up = lax.psum((d_proj, d_down_part, d_up_part), "seq")
    d_first, d_second = (
        lax.psum_scatter(d_first_part, "chan", scatter_dimension=1, tiled=True),
        lax.psum_scatter(d_second_part, "chan", scatter_dimension=1, tiled=True),
    )
    return (hidden, d_proj[:chan_rows], d_proj[chan_rows:], d_first, d_second, d_down, d_up)


def solution(mesh):
    in_specs = (
        P("chan", "seq"),
        P("chan", None),
        P("chan", None),
        P("seq", None, None),
        P("seq", None, None),
        P("chan", None),
        P("chan", None),
        P(),
        P("chan", "seq"),
    )
    out_specs = (
        P("chan", "seq"),
        P("chan", None),
        P("chan", None),
        P("seq", "chan", None),
        P("seq", "chan", None),
        P("chan", None),
        P("chan", None),
    )
    return jax.shard_map(body, mesh=mesh, in_specs=in_specs, out_specs=out_specs, check_vma=False)
```

profile of v0, /device:TPU:4, one launch (start us, length us, event | category | flops | bytes accessed | tf_op | source)
XLA Modules:
  0.0 784.1 jit_solution(4157676948622246798)
XLA Ops:
  7.2 0.0 copy-start
  7.2 0.0 all-reduce.5.cloned.1.call-start
  7.2 1.9 fusion.36
  9.1 0.0 all-reduce.5.cloned.1.call-update
  9.1 0.0 all-gather.2.cloned.1.call-start
  9.2 0.7 all-gather.2.cloned.1.call-update
  9.9 0.7 copy.46
  10.6 0.1 reduce-window.8
  10.7 0.1 reduce
  10.8 0.7 sub.6
  11.5 0.7 convert_rsqrt_fusion
  12.2 119.5 %all-reduce.5.cloned.1.call-done = f32[128,512]{1,0:T(8,128)} async-done(((f32[128,512]{1,0:T(8,128)}), f32[128,512]{1,0:T(8,128)}) %all-reduce.5.cloned.1.call-update) | async-done | bytes 262160 | tf_op jit(solution)/shard_map/psum | solution.py:34
  131.7 1.2 fusion.32
  132.9 121.2 %psum.43 = f32[64,128]{1,0:T(8,128)S(1)} all-reduce(f32[64,128]{1,0:T(8,128)S(1)} %fusion.32), channel_id=1, replica_groups=mesh['seq'=32,'chan'=16] {'seq'}, use_global_device_ids=true, to_apply=%region_2.3 | all-reduce | flops 8192 | bytes 65536 | tf_op jit(solution)/shard_map/psum | solution.py:35
  254.1 1.8 convolution_convert_fusion.4
  256.0 0.0 copy-start.5
  256.0 0.2 fusion.2
  256.2 0.8 copy.40
  257.0 25.6 %all-to-all-start = ((bf16[256,2,96]{2,1,0:T(2,128)(2,1)}), bf16[256,2,96]{2,1,0:T(2,128)(2,1)S(1)}, u32[]{:S(2)}, u32[]{:S(2)}) async-start(bf16[256,2,96]{2,1,0:T(2,128)(2,1)} %copy.40), calls=%async_computation | async-start | bytes 262144 | tf_op jit(solution)/shard_map/all_to_all | solution.py:44
  282.6 0.2 fusion.26
  282.8 9.3 %all-to-all-done = bf16[256,2,96]{2,1,0:T(2,128)(2,1)S(1)} async-done(((bf16[256,2,96]{2,1,0:T(2,128)(2,1)}), bf16[256,2,96]{2,1,0:T(2,128)(2,1)S(1)}, u32[]{:S(2)}, u32[]{:S(2)}) %all-to-all-start) | async-done | bytes 98336 | tf_op jit(solution)/shard_map/all_to_all | solution.py:44
  292.2 0.1 copy.42
  292.3 0.0 copy-done.4
  292.3 0.2 fusion.1
  292.5 0.7 copy.43
  293.3 5.7 all-to-all-start.1
  299.0 0.4 fusion.35
  299.4 8.1 %all-to-all-done.1 = bf16[8,64,96]{2,0,1:T(8,128)(2,1)S(1)} async-done(((bf16[8,64,96]{2,0,1:T(8,128)(2,1)}), bf16[8,64,96]{2,0,1:T(8,128)(2,1)S(1)}, u32[]{:S(2)}, u32[]{:S(2)}) %all-to-all-start.1) | async-done | bytes 98336 | tf_op jit(solution)/shard_map/all_to_all | solution.py:48
  307.5 0.1 copy.62
  307.6 1.0 fusion.6
  308.7 0.1 copy.47
  308.8 13.8 %all_to_all.66 = bf16[256,2,96]{2,1,0:T(2,128)(2,1)S(1)} all-to-all(bf16[256,2,96]{2,1,0:T(2,128)(2,1)S(1)} %bitcast.82), channel_id=1, replica_groups=mesh['seq'=32,'chan'=16] {'seq'}, dimensions={0} | all-to-all | bytes 196608 | tf_op jit(solution)/shard_map/all_to_all | solution.py:61
  322.7 0.1 copy.49
  322.8 0.2 fusion
  323.0 0.7 copy.51
  323.8 5.7 all-to-all-start.3
  329.5 0.0 reduce-scatter.5.cloned.1.call-start
  329.6 0.2 fusion.37
  329.8 0.9 copy.57
  330.6 0.0 reduce-scatter.5.cloned.1.call-update
  330.7 0.0 all-reduce.7.cloned.1.call-start
  330.7 7.2 all-to-all-done.3
  337.9 0.2 fusion.3
  338.2 1.7 fusion.7
  339.9 0.0 all-reduce.7.cloned.1.call-update
  339.9 0.0 all-reduce.9.cloned.1.call-start
  340.0 0.3 fusion.12
  340.3 0.1 fusion.38
  340.4 94.8 %psum.45 = f32[64,128]{1,0:T(8,128)S(1)} all-reduce(f32[64,128]{1,0:T(8,128)S(1)} %fusion.38), channel_id=1, replica_groups=mesh['seq'=32,'chan'=16] {'seq','chan'}, use_global_device_ids=true, to_apply=%region_6.7 | all-reduce | flops 8192 | bytes 65536 | tf_op jit(solution)/shard_map/psum | solution.py:75
  435.2 0.9 fusion.24
  436.2 0.4 convolution_convert_fusion.2
  436.6 0.8 convolution_bitcast_fusion
  437.4 0.0 all-reduce.9.cloned.1.call-update
  437.4 0.0 reduce-scatter.3.cloned.1.call-start
  437.4 1.0 fusion.14
  438.4 0.0 reduce-scatter.3.cloned.1.call-update
  438.5 0.0 reduce-scatter.5.cloned.1.call-done
  438.5 1.3 copy.58
  439.8 115.1 %all-reduce.7.cloned.1.call-done = f32[192,1536]{1,0:T(8,128)} async-done(((f32[192,1536]{1,0:T(8,128)}), f32[192,1536]{1,0:T(8,128)}) %all-reduce.7.cloned.1.call-update) | async-done | bytes 1179664 | tf_op jit(solution)/shard_map/psum | solution.py:84
  554.9 2.3 fusion.34
  557.2 153.8 %all-reduce.9.cloned.1.call-done = (f32[96,128]{1,0:T(8,128)}, f32[96,128]{1,0:T(8,128)}) async-done(((f32[96,128]{1,0:T(8,128)}, f32[96,128]{1,0:T(8,128)}), (f32[96,128]{1,0:T(8,128)}, f32[96,128]{1,0:T(8,128)})) %all-reduce.9.cloned.1.call-update) | async-done | bytes 98320 | tf_op jit(solution)/shard_map/psum | solution.py:84
  711.1 63.3 %reduce-scatter.3.cloned.1.call-done = f32[2,16,256]{2,1,0:T(8,128)} async-done(((f32[2,256,256]{2,1,0:T(8,128)}), f32[2,16,256]{2,1,0:T(8,128)}) %reduce-scatter.3.cloned.1.call-update) | async-done | bytes 32784 | tf_op jit(solution)/shard_map/reduce_scatter | solution.py:86
  774.4 1.4 copy.89
  775.8 1.4 copy.90
  (20 shorter events, 0.1 us)
Async XLA Ops:
  7.2 246.9 %copy-start = (bf16[96,1536]{1,0:T(8,128)(2,1)S(1)}, bf16[96,1536]{1,0:T(8,128)(2,1)}, u32[]{:S(2)}) copy-start(bf16[96,1536]{1,0:T(8,128)(2,1)} %param.11) | copy-start | bytes 884740
  7.2 248.8 %copy-start.2 = (bf16[2,256,256]{2,1,0:T(8,128)(2,1)S(1)}, bf16[2,256,256]{2,1,0:T(8,128)(2,1)}, u32[]{:S(2)}) copy-start(bf16[2,256,256]{2,1,0:T(8,128)(2,1)} %param.12) | copy-start | bytes 786436
  7.2 124.5 %all-reduce.5.cloned.1.call-start = ((), (), s32[]{:S(2)}) async-start(), calls=%async_computation.7 | async-start | bytes 524288 | tf_op jit(solution)/shard_map/psum | solution.py:34
  9.1 245.0 %all-gather.2.cloned.1.call-start = ((), (), s32[]{:S(2)}) async-start(), calls=%async_computation.6 | async-start | bytes 1671168 | tf_op jit(solution)/shard_map/all_gather | solution.py:22
  12.2 270.4 %copy-start.6 = (bf16[96,128]{1,0:T(8,128)(2,1)S(1)}, bf16[96,128]{1,0:T(8,128)(2,1)}, u32[]{:S(2)}) copy-start(bf16[96,128]{1,0:T(8,128)(2,1)} %param.15) | copy-start | bytes 73732
  254.1 38.2 %copy-start.4 = (bf16[8,64,64]{2,1,0:T(8,128)(2,1)S(1)}, bf16[8,64,64]{2,1,0:T(8,128)(2,1)}, u32[]{:S(2)}) copy-start(bf16[8,64,64]{2,1,0:T(8,128)(2,1)} %param.13) | copy-start | bytes 196612
  255.9 43.1 %copy-start.1 = (bf16[1536,512]{1,0:T(8,128)(2,1)S(1)}, bf16[1536,512]{1,0:T(8,128)(2,1)}, u32[]{:S(2)}) copy-start(bf16[1536,512]{1,0:T(8,128)(2,1)} %all-gather.2.cloned.1.call-done) | copy-start | bytes 4718596
  256.0 43.1 %copy-start.5 = (bf16[96,1536]{1,0:T(8,128)(2,1)S(1)}, bf16[96,1536]{1,0:T(8,128)(2,1)}, u32[]{:S(2)}) copy-start(bf16[96,1536]{1,0:T(8,128)(2,1)} %param.10) | copy-start | bytes 884740
  257.0 35.2 %all-to-all-start = ((bf16[256,2,96]{2,1,0:T(2,128)(2,1)}), bf16[256,2,96]{2,1,0:T(2,128)(2,1)S(1)}, u32[]{:S(2)}, u32[]{:S(2)}) async-start(bf16[256,2,96]{2,1,0:T(2,128)(2,1)} %copy.40), calls=%async_computation | async-start | bytes 262144 | tf_op jit(solution)/shard_map/all_to_all | solution.py:44
  293.3 14.4 %copy-start.7 = (bf16[96,512]{1,0:T(8,128)(2,1)S(1)}, bf16[96,512]{1,0:T(8,128)(2,1)}, u32[]{:S(2)}) copy-start(bf16[96,512]{1,0:T(8,128)(2,1)} %param.17) | copy-start | bytes 294916
  293.3 14.2 %all-to-all-start.1 = ((bf16[8,64,96]{2,0,1:T(8,128)(2,1)}), bf16[8,64,96]{2,0,1:T(8,128)(2,1)S(1)}, u32[]{:S(2)}, u32[]{:S(2)}) async-start(bf16[8,64,96]{2,0,1:T(8,128)(2,1)} %copy.43), calls=%async_computation.1 | async-start | bytes 262144 | tf_op jit(solution)/shard_map/all_to_all | solution.py:48
  323.8 14.2 %all-to-all-start.3 = ((bf16[8,64,96]{2,0,1:T(8,128)(2,1)}), bf16[8,64,96]{2,0,1:T(8,128)(2,1)S(1)}, u32[]{:S(2)}, u32[]{:S(2)}) async-start(bf16[8,64,96]{2,0,1:T(8,128)(2,1)} %copy.51), calls=%async_computation.3 | async-start | bytes 262144 | tf_op jit(solution)/shard_map/all_to_all | solution.py:66
  329.5 109.0 %reduce-scatter.5.cloned.1.call-start = ((), (), s32[]{:S(2)}) async-start(), calls=%async_computation.10 | async-start | bytes 278528 | tf_op jit(solution)/shard_map/reduce_scatter | solution.py:87
  330.7 224.3 %all-reduce.7.cloned.1.call-start = ((), (), s32[]{:S(2)}) async-start(), calls=%async_computation.8 | async-start | bytes 2359296 | tf_op jit(solution)/shard_map/psum | solution.py:84
  339.9 96.6 %copy-start.3 = (bf16[96,512]{1,0:T(8,128)(2,1)S(1)}, bf16[96,512]{1,0:T(8,128)(2,1)}, u32[]{:S(2)}) copy-start(bf16[96,512]{1,0:T(8,128)(2,1)} %param.9) | copy-start | bytes 294916
  339.9 371.1 %all-reduce.9.cloned.1.call-start = ((), (), s32[]{:S(2)}) async-start(), calls=%async_computation.11 | async-start | bytes 196608 | tf_op jit(solution)/shard_map/psum | solution.py:84
  437.4 337.0 %reduce-scatter.3.cloned.1.call-start = ((), (), s32[]{:S(2)}) async-start(), calls=%async_computation.9 | async-start | bytes 557056 | tf_op jit(solution)/shard_map/reduce_scatter | solution.py:86
Sparse Core Ops, SparseCore 0:
  10.9 120.7 all-reduce.4
  133.8 42.1 all-gather.1
  333.7 60.1 reduce-scatter.4
  397.2 157.6 all-reduce.6
  558.8 152.2 all-reduce.8
  714.3 60.0 reduce-scatter.2
where the time goes:
time: 785 us; the launch traced here: 784 us
  waiting for transfers between devices  477 us (61%)
  blocking collectives  230 us (29%)
  starting transfers between devices  37.3 us (5%)
  between operations  14.4 us (2%)
  matrix products  12.8 us (2%)
  local copies, waits for them, and re-layouts  11 us (1%)
    psum x2, waiting for transfers between devices, body(): d_proj, d_down, d_up = lax.psum((d_proj, d_down_part, d_up_part), 'seq')  269 us
    psum x1, blocking collectives, body(): lax.psum(jnp.einsum('dt,lt->dl', member, latent_full, precision=highest),...  121 us
    psum x1, waiting for transfers between devices, body(): latent_full = lax.psum(latent_part, 'chan')  120 us
    psum x1, blocking collectives, body(): lax.psum(jnp.einsum('cd,cl->dl', per_doc, up_float, precision=highest), (...  94.8 us
    reduce_scatter x1, waiting for transfers between devices, body(): lax.psum_scatter(d_first_part, 'chan', scatter_dimension=1, tiled=True)  63.3 us
    all_to_all x1, starting transfers between devices, body(): lax.all_to_all(inner_mix, 'seq', split_axis=0, concat_axis=1, tiled=True)  25.6 us
  transfers between devices with their start and end apart: 9, of which 7 were waited for; matrix products, arithmetic and copies ran while one was open for 2% of the time, Pallas kernels for 0%

commit v1 on v0

--- a/solution.py
+++ b/solution.py
@@ -31,7 +31,11 @@
     ).astype(jnp.float32)
     len_scale = lax.rsqrt(doc_lengths.astype(jnp.float32))
     latent_part = jnp.einsum("ct,cl->lt", tokens, down_latent, preferred_element_type=jnp.float32)
-    latent_full = lax.psum(latent_part, "chan")
+    latent_full = latent_part
+    for hop in (1, 2, 4, 8):
+        latent_full = latent_full + lax.ppermute(
+            latent_full, "chan", [(dev, dev ^ hop) for dev in range(16)]
+        )
     doc_sums = lax.psum(jnp.einsum("dt,lt->dl", member, latent_full, precision=highest), "seq")
     pooled = doc_sums * len_scale[:, None]
     up_float = up_latent.astype(jnp.float32)

time: 785 us -> 718 us (0.915)
  waiting for transfers between devices: 477 us -> 390 us
  starting transfers between devices: 37.3 us -> 59 us
    psum x1 -> x0, waiting for transfers between devices: 120 us -> none  [body(): latent_full = lax.psum(latent_part, 'chan')]
    ppermute x0 -> x4, waiting for transfers between devices: none -> 35.7 us  [body(): lax.ppermute(latent_full, 'chan', [(dev, dev ^ hop) for dev in range(16)])]
    ppermute x0 -> x4, starting transfers between devices: none -> 21.5 us  [body(): lax.ppermute(latent_full, 'chan', [(dev, dev ^ hop) for dev in range(16)])]
  transfers between devices with their start and end apart: 9 -> 12, of which waited for: 7 -> 10; matrix products, arithmetic and copies ran while one was open for 2% -> 2% of each run, Pallas kernels for 0% -> 0%
where the time goes in v1:
time: 718 us; the launch traced here: 717 us
  waiting for transfers between devices  390 us (54%)
  blocking collectives  232 us (32%)
  starting transfers between devices  59 us (8%)
  between operations  14.1 us (2%)
  matrix products  11.1 us (2%)
  local copies, waits for them, and re-layouts  10.4 us (1%)
    psum x2, waiting for transfers between devices, body(): d_proj, d_down, d_up = lax.psum((d_proj, d_down_part, d_up_part), 'seq')  266 us
    psum x1, blocking collectives, body(): lax.psum(jnp.einsum('dt,lt->dl', member, latent_full, precision=highest),...  120 us
    psum x1, blocking collectives, body(): lax.psum(jnp.einsum('cd,cl->dl', per_doc, up_float, precision=highest), (...  97.9 us
    reduce_scatter x1, waiting for transfers between devices, body(): lax.psum_scatter(d_first_part, 'chan', scatter_dimension=1, tiled=True)  63.3 us
    ppermute x4, waiting for transfers between devices, body(): lax.ppermute(latent_full, 'chan', [(dev, dev ^ hop) for dev in range(16)])  35.7 us
    all_to_all x1, starting transfers between devices, body(): lax.all_to_all(inner_mix, 'seq', split_axis=0, concat_axis=1, tiled=True)  25.6 us
    ppermute x4, starting transfers between devices, body(): lax.ppermute(latent_full, 'chan', [(dev, dev ^ hop) for dev in range(16)])  21.5 us
  transfers between devices with their start and end apart: 12, of which 10 were waited for; matrix products, arithmetic and copies ran while one was open for 2% of the time, Pallas kernels for 0%

profile of v1, /device:TPU:4, one launch (start us, length us, event | category | flops | bytes accessed | tf_op | source)
XLA Modules:
  0.0 716.8 jit_solution(15706634086214429005)
XLA Ops:
  7.2 0.0 all-gather.2.cloned.1.call-start
  7.2 0.7 all-gather.2.cloned.1.call-update
  7.9 1.1 fusion.37
  9.0 1.9 collective-permute-start
  11.0 1.5 collective-permute-done
  12.5 4.3 collective-permute-start.1
  16.8 6.6 collective-permute-done.1
  23.4 6.1 collective-permute-start.2
  29.5 15.0 %collective-permute-done.2 = f32[128,512]{1,0:T(8,128)S(1)} collective-permute-done((f32[128,512]{1,0:T(8,128)S(1)}, f32[128,512]{1,0:T(8,128)S(1)}, u32[]{:S(2)}, u32[]{:S(2)}) %collective-permute-start.2) | collective-permute-done | bytes 262176 | tf_op jit(solution)/shard_map/ppermute | solution.py:36
  44.6 9.2 %collective-permute-start.3 = (f32[128,512]{1,0:T(8,128)S(1)}, f32[128,512]{1,0:T(8,128)S(1)}, u32[]{:S(2)}, u32[]{:S(2)}) collective-permute-start(f32[128,512]{1,0:T(8,128)S(1)} %add.50), channel_id=1, source_target_pairs={{0,8},{1,9},{2,10},{3,11},{4,12},{5,13},{6,14},{7,15},{8,0},{9,1},... | collective-permute-start | bytes 786440 | tf_op jit(solution)/shard_map/ppermute | solution.py:36
  53.8 0.1 copy.46
  53.9 0.1 reduce-window.8
  54.0 0.1 reduce
  54.1 12.6 %collective-permute-done.3 = f32[128,512]{1,0:T(8,128)S(1)} collective-permute-done((f32[128,512]{1,0:T(8,128)S(1)}, f32[128,512]{1,0:T(8,128)S(1)}, u32[]{:S(2)}, u32[]{:S(2)}) %collective-permute-start.3) | collective-permute-done | bytes 262176 | tf_op jit(solution)/shard_map/ppermute | solution.py:36
  66.8 0.3 fusion.4
  67.1 120.5 %psum.35 = f32[64,128]{1,0:T(8,128)S(1)} all-reduce(f32[64,128]{1,0:T(8,128)S(1)} %fusion.4), channel_id=1, replica_groups=mesh['seq'=32,'chan'=16] {'seq'}, use_global_device_ids=true, to_apply=%region_1.2 | all-reduce | flops 8192 | bytes 65536 | tf_op jit(solution)/shard_map/psum | solution.py:39
  187.6 1.8 convolution_convert_fusion.4
  189.4 0.2 fusion.2
  189.6 0.8 copy.40
  190.4 25.6 %all-to-all-start = ((bf16[256,2,96]{2,1,0:T(2,128)(2,1)}), bf16[256,2,96]{2,1,0:T(2,128)(2,1)S(1)}, u32[]{:S(2)}, u32[]{:S(2)}) async-start(bf16[256,2,96]{2,1,0:T(2,128)(2,1)} %copy.40), calls=%async_computation | async-start | bytes 262144 | tf_op jit(solution)/shard_map/all_to_all | solution.py:48
  216.1 0.2 fusion.28
  216.3 8.2 %all-to-all-done = bf16[256,2,96]{2,1,0:T(2,128)(2,1)S(1)} async-done(((bf16[256,2,96]{2,1,0:T(2,128)(2,1)}), bf16[256,2,96]{2,1,0:T(2,128)(2,1)S(1)}, u32[]{:S(2)}, u32[]{:S(2)}) %all-to-all-start) | async-done | bytes 98336 | tf_op jit(solution)/shard_map/all_to_all | solution.py:48
  224.5 0.1 copy.42
  224.7 0.2 fusion.1
  224.9 0.7 copy.43
  225.6 5.9 all-to-all-start.1
  231.6 0.4 fusion.36
  231.9 8.1 %all-to-all-done.1 = bf16[8,64,96]{2,0,1:T(8,128)(2,1)S(1)} async-done(((bf16[8,64,96]{2,0,1:T(8,128)(2,1)}), bf16[8,64,96]{2,0,1:T(8,128)(2,1)S(1)}, u32[]{:S(2)}, u32[]{:S(2)}) %all-to-all-start.1) | async-done | bytes 98336 | tf_op jit(solution)/shard_map/all_to_all | solution.py:52
  240.0 0.1 copy.62
  240.2 1.0 fusion.8
  241.2 0.1 copy.47
  241.4 13.8 %all_to_all.66 = bf16[256,2,96]{2,1,0:T(2,128)(2,1)S(1)} all-to-all(bf16[256,2,96]{2,1,0:T(2,128)(2,1)S(1)} %bitcast.81), channel_id=1, replica_groups=mesh['seq'=32,'chan'=16] {'seq'}, dimensions={0} | all-to-all | bytes 196608 | tf_op jit(solution)/shard_map/all_to_all | solution.py:65
  255.2 0.1 copy.49
  255.3 0.2 fusion
  255.6 0.7 copy.51
  256.3 5.7 all-to-all-start.3
  262.1 0.0 reduce-scatter.5.cloned.1.call-start
  262.1 0.2 fusion.38
  262.3 0.9 copy.57
  263.2 0.0 reduce-scatter.5.cloned.1.call-update
  263.2 0.0 all-reduce.4.cloned.1.call-start
  263.2 7.2 %all-to-all-done.3 = bf16[8,64,96]{2,0,1:T(8,128)(2,1)S(1)} async-done(((bf16[8,64,96]{2,0,1:T(8,128)(2,1)}), bf16[8,64,96]{2,0,1:T(8,128)(2,1)S(1)}, u32[]{:S(2)}, u32[]{:S(2)}) %all-to-all-start.3) | async-done | bytes 98336 | tf_op jit(solution)/shard_map/all_to_all | solution.py:70
  270.5 0.2 fusion.3
  270.7 1.7 fusion.9
  272.4 0.0 all-reduce.4.cloned.1.call-update
  272.4 0.0 all-reduce.6.cloned.1.call-start
  272.5 0.3 fusion.14
  272.8 0.1 fusion.39
  273.0 97.9 %psum.37 = f32[64,128]{1,0:T(8,128)S(1)} all-reduce(f32[64,128]{1,0:T(8,128)S(1)} %fusion.39), channel_id=1, replica_groups=mesh['seq'=32,'chan'=16] {'seq','chan'}, use_global_device_ids=true, to_apply=%region_5.6 | all-reduce | flops 8192 | bytes 65536 | tf_op jit(solution)/shard_map/psum | solution.py:79
  370.8 0.9 fusion.26
  371.7 0.4 convolution_convert_fusion.2
  372.1 0.8 convolution_bitcast_fusion
  372.9 0.0 all-reduce.6.cloned.1.call-update
  372.9 0.0 reduce-scatter.3.cloned.1.call-start
  373.0 1.0 fusion.16
  374.0 0.0 reduce-scatter.3.cloned.1.call-update
  374.0 0.0 reduce-scatter.5.cloned.1.call-done
  374.1 1.3 copy.58
  375.4 112.5 %all-reduce.4.cloned.1.call-done = f32[192,1536]{1,0:T(8,128)} async-done(((f32[192,1536]{1,0:T(8,128)}), f32[192,1536]{1,0:T(8,128)}) %all-reduce.4.cloned.1.call-update) | async-done | bytes 1179664 | tf_op jit(solution)/shard_map/psum | solution.py:88
  487.9 2.3 fusion.35
  490.3 153.8 %all-reduce.6.cloned.1.call-done = (f32[96,128]{1,0:T(8,128)}, f32[96,128]{1,0:T(8,128)}) async-done(((f32[96,128]{1,0:T(8,128)}, f32[96,128]{1,0:T(8,128)}), (f32[96,128]{1,0:T(8,128)}, f32[96,128]{1,0:T(8,128)})) %all-reduce.6.cloned.1.call-update) | async-done | bytes 98320 | tf_op jit(solution)/shard_map/psum | solution.py:88
  644.1 63.3 %reduce-scatter.3.cloned.1.call-done = f32[2,16,256]{2,1,0:T(8,128)} async-done(((f32[2,256,256]{2,1,0:T(8,128)}), f32[2,16,256]{2,1,0:T(8,128)}) %reduce-scatter.3.cloned.1.call-update) | async-done | bytes 32784 | tf_op jit(solution)/shard_map/reduce_scatter | solution.py:90
  707.4 1.4 copy.88
  708.8 1.4 copy.89
  (30 shorter events, 0.3 us)
Async XLA Ops:
  7.2 180.4 %copy-start = (bf16[96,1536]{1,0:T(8,128)(2,1)S(1)}, bf16[96,1536]{1,0:T(8,128)(2,1)}, u32[]{:S(2)}) copy-start(bf16[96,1536]{1,0:T(8,128)(2,1)} %param.11) | copy-start | bytes 884740
  7.2 46.6 %copy-start.7 = (s32[64]{0:T(128)S(1)}, s32[64]{0:T(128)}, u32[]{:S(2)}) copy-start(s32[64]{0:T(128)} %param.16) | copy-start | bytes 772
  7.2 180.4 %all-gather.2.cloned.1.call-start = ((), (), s32[]{:S(2)}) async-start(), calls=%async_computation.6 | async-start | bytes 1671168 | tf_op jit(solution)/shard_map/all_gather | solution.py:22
  9.0 3.4 collective-permute-start
  12.5 10.9 %collective-permute-start.1 = (f32[128,512]{1,0:T(8,128)S(1)}, f32[128,512]{1,0:T(8,128)S(1)}, u32[]{:S(2)}, u32[]{:S(2)}) collective-permute-start(f32[128,512]{1,0:T(8,128)S(1)} %add.48), channel_id=1, source_target_pairs={{0,2},{1,3},{2,0},{3,1},{4,6},{5,7},{6,4},{7,5},{8,10},{9,11},{10,... | collective-permute-start | bytes 786440 | tf_op jit(solution)/shard_map/ppermute | solution.py:36
  23.4 21.1 %collective-permute-start.2 = (f32[128,512]{1,0:T(8,128)S(1)}, f32[128,512]{1,0:T(8,128)S(1)}, u32[]{:S(2)}, u32[]{:S(2)}) collective-permute-start(f32[128,512]{1,0:T(8,128)S(1)} %add.49), channel_id=1, source_target_pairs={{0,4},{1,5},{2,6},{3,7},{4,0},{5,1},{6,2},{7,3},{8,12},{9,13},{10,... | collective-permute-start | bytes 786440 | tf_op jit(solution)/shard_map/ppermute | solution.py:36
  29.5 159.9 %copy-start.2 = (bf16[2,256,256]{2,1,0:T(8,128)(2,1)S(1)}, bf16[2,256,256]{2,1,0:T(8,128)(2,1)}, u32[]{:S(2)}) copy-start(bf16[2,256,256]{2,1,0:T(8,128)(2,1)} %param.12) | copy-start | bytes 786436
  44.6 22.2 %collective-permute-start.3 = (f32[128,512]{1,0:T(8,128)S(1)}, f32[128,512]{1,0:T(8,128)S(1)}, u32[]{:S(2)}, u32[]{:S(2)}) collective-permute-start(f32[128,512]{1,0:T(8,128)S(1)} %add.50), channel_id=1, source_target_pairs={{0,8},{1,9},{2,10},{3,11},{4,12},{5,13},{6,14},{7,15},{8,0},{9,1},... | collective-permute-start | bytes 786440 | tf_op jit(solution)/shard_map/ppermute | solution.py:36
  67.1 149.0 %copy-start.6 = (bf16[96,128]{1,0:T(8,128)(2,1)S(1)}, bf16[96,128]{1,0:T(8,128)(2,1)}, u32[]{:S(2)}) copy-start(bf16[96,128]{1,0:T(8,128)(2,1)} %param.15) | copy-start | bytes 73732
  187.5 37.1 %copy-start.4 = (bf16[8,64,64]{2,1,0:T(8,128)(2,1)S(1)}, bf16[8,64,64]{2,1,0:T(8,128)(2,1)}, u32[]{:S(2)}) copy-start(bf16[8,64,64]{2,1,0:T(8,128)(2,1)} %param.13) | copy-start | bytes 196612
  189.4 42.2 %copy-start.1 = (bf16[1536,512]{1,0:T(8,128)(2,1)S(1)}, bf16[1536,512]{1,0:T(8,128)(2,1)}, u32[]{:S(2)}) copy-start(bf16[1536,512]{1,0:T(8,128)(2,1)} %all-gather.2.cloned.1.call-done) | copy-start | bytes 4718596
  189.4 42.2 %copy-start.5 = (bf16[96,1536]{1,0:T(8,128)(2,1)S(1)}, bf16[96,1536]{1,0:T(8,128)(2,1)}, u32[]{:S(2)}) copy-start(bf16[96,1536]{1,0:T(8,128)(2,1)} %param.10) | copy-start | bytes 884740
  190.4 34.1 %all-to-all-start = ((bf16[256,2,96]{2,1,0:T(2,128)(2,1)}), bf16[256,2,96]{2,1,0:T(2,128)(2,1)S(1)}, u32[]{:S(2)}, u32[]{:S(2)}) async-start(bf16[256,2,96]{2,1,0:T(2,128)(2,1)} %copy.40), calls=%async_computation | async-start | bytes 262144 | tf_op jit(solution)/shard_map/all_to_all | solution.py:48
  225.6 14.6 %copy-start.8 = (bf16[96,512]{1,0:T(8,128)(2,1)S(1)}, bf16[96,512]{1,0:T(8,128)(2,1)}, u32[]{:S(2)}) copy-start(bf16[96,512]{1,0:T(8,128)(2,1)} %param.17) | copy-start | bytes 294916
  225.6 14.4 %all-to-all-start.1 = ((bf16[8,64,96]{2,0,1:T(8,128)(2,1)}), bf16[8,64,96]{2,0,1:T(8,128)(2,1)S(1)}, u32[]{:S(2)}, u32[]{:S(2)}) async-start(bf16[8,64,96]{2,0,1:T(8,128)(2,1)} %copy.43), calls=%async_computation.1 | async-start | bytes 262144 | tf_op jit(solution)/shard_map/all_to_all | solution.py:52
  256.3 14.2 %all-to-all-start.3 = ((bf16[8,64,96]{2,0,1:T(8,128)(2,1)}), bf16[8,64,96]{2,0,1:T(8,128)(2,1)S(1)}, u32[]{:S(2)}, u32[]{:S(2)}) async-start(bf16[8,64,96]{2,0,1:T(8,128)(2,1)} %copy.51), calls=%async_computation.3 | async-start | bytes 262144 | tf_op jit(solution)/shard_map/all_to_all | solution.py:70
  262.1 112.0 %reduce-scatter.5.cloned.1.call-start = ((), (), s32[]{:S(2)}) async-start(), calls=%async_computation.9 | async-start | bytes 278528 | tf_op jit(solution)/shard_map/reduce_scatter | solution.py:91
  263.2 224.7 %all-reduce.4.cloned.1.call-start = ((), (), s32[]{:S(2)}) async-start(), calls=%async_computation.7 | async-start | bytes 2359296 | tf_op jit(solution)/shard_map/psum | solution.py:88
  272.4 99.7 %copy-start.3 = (bf16[96,512]{1,0:T(8,128)(2,1)S(1)}, bf16[96,512]{1,0:T(8,128)(2,1)}, u32[]{:S(2)}) copy-start(bf16[96,512]{1,0:T(8,128)(2,1)} %param.9) | copy-start | bytes 294916
  272.4 371.6 %all-reduce.6.cloned.1.call-start = ((), (), s32[]{:S(2)}) async-start(), calls=%async_computation.10 | async-start | bytes 196608 | tf_op jit(solution)/shard_map/psum | solution.py:88
  372.9 334.5 %reduce-scatter.3.cloned.1.call-start = ((), (), s32[]{:S(2)}) async-start(), calls=%async_computation.8 | async-start | bytes 557056 | tf_op jit(solution)/shard_map/reduce_scatter | solution.py:90
Sparse Core Ops, SparseCore 0:
  10.1 55.1 all-gather.1
  266.2 60.4 reduce-scatter.4
  330.1 157.7 all-reduce.3
  491.8 152.2 all-reduce.5
  647.3 60.0 reduce-scatter.2
